TPU v7x, 128 devices: a whole 4x4x4 slice. The times are simulated.
128 devices in a mesh: island: 8 (over z, x_lo), fsdp: 16 (over x_hi, y, core).
Axes of the slice: x: 4 (x_hi: 2, x_lo: 2; x = x_hi * 2 + x_lo), y: 4, z: 4, core: 2. Of those that a mesh axis runs over, the one named last changes fastest.
Arguments:
- tokens: bfloat16 [8, 8192, 8192], P('island', 'fsdp'), may hold values from -6 to 6
- key_grad_out: bfloat16 [8, 8192, 1024], P('island', 'fsdp'), may hold values from -0.0625 to 0.0625
- key_master: float32 [8, 8192, 1024], P('island', 'fsdp'), may hold values from -0.0625 to 0.0625
- key_first: float32 [8, 8192, 1024], P('island', 'fsdp'), may hold values from -4 to 4
- key_second: float32 [8, 8192, 1024], P('island', 'fsdp'), may hold values from 0.05 to 2
- frag_local: float32 [8, 8192, 1024], P('island', 'fsdp'), may hold values from -1.5 to 1.5
- frag_anchor: float32 [8192, 1024], P('fsdp'), may hold values from -1.5 to 1.5
- frag_momentum: float32 [8192, 1024], P('fsdp'), may hold values from -1.5 to 1.5
Outputs:
- new_master: float32 [8, 8192, 1024], P('island', 'fsdp')
- new_first: float32 [8, 8192, 1024], P('island', 'fsdp')
- new_second: float32 [8, 8192, 1024], P('island', 'fsdp')
- next_keys: float32 [8, 8192, 1024], P('island', 'fsdp')
- new_anchor: float32 [8192, 1024], P('fsdp')
- new_momentum: float32 [8192, 1024], P('fsdp')
All inputs are finite; a program needn't handle non-finite values.
Results may differ from a plain program's by a relative error of at most 0.0029.
Values may be sent and summed in bfloat16 or wider, within the bound.
No kernel may reach another device: no remote copies, remote signals or barrier semaphores. Data moves between devices by JAX's collectives and lax.ppermute only.
A program may use at most 192 MiB of HBM per device.

v0:
```python
import jax
import jax.numpy as jnp
from jax import lax
from jax.sharding import PartitionSpec as P

BETA_ONE = 0.9
BETA_TWO = 0.95
INNER_RATE = 0.002
DECAY_RATE = 0.1
EPSILON = 1e-08
OUTER_RATE = 0.7
OUTER_MOMENT = 0.9


def outer_update(outer_grad, anchor_rows, momentum_rows):
    momentum_new = OUTER_MOMENT * momentum_rows + outer_grad
    anchor_new = anchor_rows - OUTER_RATE * (outer_grad + OUTER_MOMENT * momentum_new)
    return (anchor_new, momentum_new)


def per_device(
    tokens, key_grad_out, key_master, key_first, key_second, frag_local, frag_anchor, frag_momentum
):
    activations = tokens[0]
    upstream = key_grad_out[0]
    master = key_master[0]
    feature_slab = activations
    grad = lax.psum_scatter(
        lax.dot_general(
            feature_slab, upstream, (((0,), (0,)), ((), ())), preferred_element_type=jnp.float32
        ),
        "fsdp",
        scatter_dimension=0,
        tiled=True,
    )
    first_new = BETA_ONE * key_first[0] + (1.0 - BETA_ONE) * grad
    second_new = BETA_TWO * key_second[0] + (1.0 - BETA_TWO) * grad * grad
    update = first_new / (jnp.sqrt(second_new) + EPSILON)
    master_new = master - INNER_RATE * (update + DECAY_RATE * master)
    weight_bf = master_new.astype(jnp.bfloat16)
    feature_slab = activations
    key_values = jnp.dot(
        feature_slab,
        lax.all_gather(weight_bf, "fsdp", axis=0, tiled=True),
        preferred_element_type=jnp.float32,
    )
    island_count = lax.axis_size("island")
    pseudo = frag_anchor - frag_local[0]
    summed = lax.psum(pseudo, "island")
    new_anchor, new_momentum = outer_update(summed / island_count, frag_anchor, frag_momentum)
    return (
        master_new[None],
        first_new[None],
        second_new[None],
        key_values[None],
        new_anchor,
        new_momentum,
    )


def solution(mesh):
    return jax.shard_map(
        per_device,
        mesh=mesh,
        in_specs=(
            P("island", "fsdp", None),
            P("island", "fsdp", None),
            P("island", "fsdp", None),
            P("island", "fsdp", None),
            P("island", "fsdp", None),
            P("island", "fsdp", None),
            P("fsdp", None),
            P("fsdp", None),
        ),
        out_specs=(
            P("island", "fsdp", None),
            P("island", "fsdp", None),
            P("island", "fsdp", None),
            P("island", "fsdp", None),
            P("fsdp", None),
            P("fsdp", None),
        ),
        check_vma=False,
    )
```

profile of v0, /device:TPU:1, one launch (start us, length us, event | category | flops | bytes accessed | tf_op | source)
XLA Modules:
  0.0 440.7 jit_solution(17716569214304781898)
XLA Ops:
  8.0 0.0 copy-start
  8.0 0.0 reduce-scatter.2.cloned.1.call-start
  8.1 1.2 copy-done
  9.2 18.7 %fusion.2 = f32[8192,1024]{1,0:T(8,128)} fusion(bf16[1,512,8192]{2,1,0:T(8,128)(2,1)} %param.8, bf16[1,512,1024]{2,1,0:T(8,128)(2,1)S(1)} %copy-done), kind=kOutput, calls=%fused_computation.2 | convolution fusion | flops 8589934592 | bytes 42991616 | tf_op jit(solution)/shard_map/dot_general | solution.py:29
  28.0 0.0 copy-start.2
  28.0 0.0 reduce-scatter.2.cloned.1.call-update
  28.0 0.0 all-reduce.2.cloned.1.call-start
  28.0 1.5 copy-done.2
  29.6 3.5 bitcast_subtract_fusion
  33.0 0.0 all-reduce.2.cloned.1.call-update
  33.0 0.2 all-gather.2.cloned.1.call-start
  33.3 260.7 %reduce-scatter.2.cloned.1.call-done = f32[512,1024]{1,0:T(8,128)} async-done(((f32[8192,1024]{1,0:T(8,128)}), f32[512,1024]{1,0:T(8,128)}) %reduce-scatter.2.cloned.1.call-update) | async-done | bytes 2097168 | tf_op jit(solution)/shard_map/reduce_scatter | solution.py:28
  294.0 8.3 %fusion.13 = (bf16[512,1024]{1,0:T(8,128)(2,1)}, f32[512,1024]{1,0:T(8,128)}, f32[1,512,1024]{2,1,0:T(8,128)}, f32[1,512,1024]{2,1,0:T(8,128)}) fusion(f32[512,1024]{1,0:T(8,128)} %reduce-scatter.2.cloned.1.call-done, f32[1,512,1024]{2,1,0:T(8,128)} %param.12, f32[1,512,1024]{2,1,0:T(8,128)} %param.11, f32[1,512,1024]{2,1,0:T(8,128)} %param.10), kind=kLoop, calls=%fused_computation.18 | loop fusion | flops 7340032 | bytes 15728640 | tf_op jit(solution)/shard_map/convert_element_type | solution.py:40
  302.3 0.0 all-gather.2.cloned.1.call-update
  302.3 0.0 all-reduce.2.cloned.1.call-done
  302.3 5.5 %multiply_subtract_fusion = (f32[512,1024]{1,0:T(8,128)}, f32[512,1024]{1,0:T(8,128)}) fusion(f32[512,1024]{1,0:T(8,128)S(1)} %copy-done.2, f32[512,1024]{1,0:T(8,128)} %all-reduce.2.cloned.1.call-done, f32[512,1024]{1,0:T(8,128)} %param.15), kind=kLoop, calls=%fused_computation.12 | loop fusion | flops 3670016 | bytes 10485760 | tf_op jit(solution)/shard_map/sub | solution.py:17
  307.8 106.6 %all-gather.2.cloned.1.call-done = bf16[8192,1024]{1,0:T(8,128)(2,1)} async-done(((bf16[512,1024]{1,0:T(8,128)(2,1)}), bf16[8192,1024]{1,0:T(8,128)(2,1)}) %all-gather.2.cloned.1.call-update) | async-done | bytes 16777232 | tf_op jit(solution)/shard_map/all_gather | solution.py:44
  414.4 0.0 copy-start.1
  414.4 16.0 %fusion.7 = f32[1,512,1024]{1,2,0:T(8,128)} fusion(bf16[8192,1024]{1,0:T(8,128)(2,1)} %all-gather.2.cloned.1.call-done, bf16[1,512,8192]{2,1,0:T(8,128)(2,1)} %param.8), kind=kOutput, calls=%fused_computation.14 | convolution fusion | flops 8589934592 | bytes 27262976 | tf_op jit(solution)/shard_map/dot_general | solution.py:42
  430.4 2.9 copy.14
  433.3 0.0 copy-done.1
Async XLA Ops:
  8.0 1.2 copy-start
  8.0 285.9 %reduce-scatter.2.cloned.1.call-start = ((), (), s32[]{:S(2)}) async-start(), calls=%async_computation.1 | async-start | bytes 35651584 | tf_op jit(solution)/shard_map/reduce_scatter | solution.py:28
  28.0 1.6 copy-start.2
  28.0 274.3 %all-reduce.2.cloned.1.call-start = ((), (), s32[]{:S(2)}) async-start(), calls=%async_computation.3 | async-start | bytes 4194304 | tf_op jit(solution)/shard_map/psum | solution.py:49
  33.0 381.4 %all-gather.2.cloned.1.call-start = ((), (), s32[]{:S(2)}) async-start(), calls=%async_computation.2 | async-start | bytes 17825792 | tf_op jit(solution)/shard_map/all_gather | solution.py:44
  414.4 18.9 %copy-start.1 = (bf16[1,512,1024]{2,1,0:T(8,128)(2,1)S(1)}, bf16[1,512,1024]{2,1,0:T(8,128)(2,1)}, u32[]{:S(2)}) copy-start(bf16[1,512,1024]{2,1,0:T(8,128)(2,1)} %param.9) | copy-start | bytes 3145732
Sparse Core Ops, SparseCore 0:
  28.1 265.8 reduce-scatter.1
  302.4 111.9 all-gather.1
Sparse Core Ops, SparseCore 1:
  33.1 140.4 all-reduce.1
where the time goes:
time: 441 us
  waiting for transfers between devices  367 us (83%)
  matrix products  34.7 us (8%)
  other arithmetic  17.2 us (4%)
  between operations  15.5 us (4%)
  local copies, waits for them, and re-layouts  5.58 us (1%)
    reduce_scatter x1, waiting for transfers between devices, per_device(): lax.psum_scatter(lax.dot_general(feature_slab, upstream, (((0,), (0,)), (...  261 us
    all_gather x1, waiting for transfers between devices, per_device(): lax.all_gather(weight_bf, 'fsdp', axis=0, tiled=True)  107 us
    dot_general x1, matrix products, per_device(): lax.dot_general(feature_slab, upstream, (((0,), (0,)), ((), ())), preferr...  18.7 us
    dot_general x1, matrix products, per_device(): jnp.dot(feature_slab, lax.all_gather(weight_bf, 'fsdp', axis=0, tiled=Tru...  16 us
  transfers between devices with their start and end apart: 3, of which 2 were waited for; matrix products, arithmetic and copies ran while one was open for 4% of the time, Pallas kernels for 0%

commit v1 on v0

--- a/solution.py
+++ b/solution.py
@@ -41,7 +41,9 @@
     feature_slab = activations
     key_values = jnp.dot(
         feature_slab,
-        lax.all_gather(weight_bf, "fsdp", axis=0, tiled=True),
+        jnp.concatenate(
+            lax.all_to_all(jnp.stack([weight_bf] * lax.axis_size("fsdp")), "fsdp", 0, 0), axis=0
+        ),
         preferred_element_type=jnp.float32,
     )
     island_count = lax.axis_size("island")

time: 441 us -> 629 us (1.43)
  the two profiles are of different devices: /device:TPU:1 before, /device:TPU:25 now
where the time goes in v1:
time: 629 us
  waiting for transfers between devices  546 us (87%)
  matrix products  33.1 us (5%)
  between operations  15.5 us (2%)
  other arithmetic  15.3 us (2%)
  starting transfers between devices  9.65 us (2%)
  local copies, waits for them, and re-layouts  8.97 us (1%)
    reduce_scatter x1, waiting for transfers between devices, per_device(): lax.psum_scatter(lax.dot_general(feature_slab, upstream, (((0,), (0,)), (...  246 us
    psum x1, waiting for transfers between devices, per_device(): summed = lax.psum(pseudo, 'island')  184 us
    all_to_all x1, waiting for transfers between devices, per_device(): lax.all_to_all(jnp.stack([weight_bf] * lax.axis_size('fsdp')), 'fsdp', 0, 0)  116 us
    dot_general x1, matrix products, per_device(): lax.dot_general(feature_slab, upstream, (((0,), (0,)), ((), ())), preferr...  18.7 us
    dot_general x1, matrix products, per_device(): jnp.dot(feature_slab, jnp.concatenate(lax.all_to_all(jnp.stack([weight_bf...  14.3 us
  transfers between devices with their start and end apart: 3, of which 3 were waited for; matrix products, arithmetic and copies ran while one was open for 1% of the time, Pallas kernels for 0%

profile of v1, /device:TPU:25, one launch (start us, length us, event | category | flops | bytes accessed | tf_op | source)
XLA Modules:
  0.0 628.6 jit_solution(13623876286576059405)
XLA Ops:
  8.0 0.0 copy-start
  8.0 0.0 reduce-scatter.2.cloned.1.call-start
  8.1 1.2 copy-done
  9.2 18.7 %fusion.2 = f32[8192,1024]{1,0:T(8,128)} fusion(bf16[1,512,8192]{2,1,0:T(8,128)(2,1)} %param.8, bf16[1,512,1024]{2,1,0:T(8,128)(2,1)S(1)} %copy-done), kind=kOutput, calls=%fused_computation.2 | convolution fusion | flops 8589934592 | bytes 42991616 | tf_op jit(solution)/shard_map/dot_general | solution.py:29
  28.0 0.0 copy-start.3
  28.0 0.0 reduce-scatter.2.cloned.1.call-update
  28.0 245.7 %reduce-scatter.2.cloned.1.call-done = f32[512,1024]{1,0:T(8,128)} async-done(((f32[8192,1024]{1,0:T(8,128)}), f32[512,1024]{1,0:T(8,128)}) %reduce-scatter.2.cloned.1.call-update) | async-done | bytes 2097168 | tf_op jit(solution)/shard_map/reduce_scatter | solution.py:28
  273.7 0.0 copy-done.3
  273.7 6.7 %fusion.13 = (bf16[512,1024]{1,0:T(8,128)(2,1)S(1)}, f32[512,1024]{1,0:T(8,128)}, f32[1,512,1024]{2,1,0:T(8,128)}, f32[1,512,1024]{2,1,0:T(8,128)}) fusion(f32[512,1024]{1,0:T(8,128)} %reduce-scatter.2.cloned.1.call-done, f32[1,512,1024]{2,1,0:T(8,128)S(1)} %copy-done.3, f32[1,512,1024]{2,1,0:T(8,128)} %param.11, f32[1,512,1024]{2,1,0:T(8,128)} %param.10), kind=kLoop, calls=%fused_computation.18 | loop fusion | flops 7340032 | bytes 15728640 | tf_op jit(solution)/shard_map/convert_element_type | solution.py:40
  280.4 6.0 stack.2
  286.4 0.0 copy-start.2
  286.4 9.6 %all-to-all-start = ((bf16[16,512,1024]{2,1,0:T(8,128)(2,1)}), bf16[16,512,1024]{2,1,0:T(8,128)(2,1)}, u32[]{:S(2)}, u32[]{:S(2)}) async-start(bf16[16,512,1024]{2,1,0:T(8,128)(2,1)} %stack.2), calls=%async_computation.1 | async-start | bytes 33554432 | tf_op jit(solution)/shard_map/all_to_all | solution.py:45
  296.0 0.0 all-reduce.2.cloned.1.call-start
  296.0 0.0 copy-done.2
  296.0 3.3 bitcast_subtract_fusion
  299.3 0.0 all-reduce.2.cloned.1.call-update
  299.3 184.4 %all-reduce.2.cloned.1.call-done = f32[512,1024]{1,0:T(8,128)} async-done(((f32[512,1024]{1,0:T(8,128)}), f32[512,1024]{1,0:T(8,128)}) %all-reduce.2.cloned.1.call-update) | async-done | bytes 2097168 | tf_op jit(solution)/shard_map/psum | solution.py:51
  483.7 5.2 multiply_subtract_fusion
  488.9 116.1 %all-to-all-done = bf16[16,512,1024]{2,1,0:T(8,128)(2,1)} async-done(((bf16[16,512,1024]{2,1,0:T(8,128)(2,1)}), bf16[16,512,1024]{2,1,0:T(8,128)(2,1)}, u32[]{:S(2)}, u32[]{:S(2)}) %all-to-all-start) | async-done | bytes 16777248 | tf_op jit(solution)/shard_map/all_to_all | solution.py:45
  605.0 0.0 copy-start.1
  605.0 14.3 %fusion.7 = f32[1,512,1024]{1,2,0:T(8,128)S(1)} fusion(bf16[8192,1024]{1,0:T(8,128)(2,1)} %bitcast.8, bf16[1,512,8192]{2,1,0:T(8,128)(2,1)} %param.8), kind=kOutput, calls=%fused_computation.14 | convolution fusion | flops 8589934592 | bytes 27262976 | tf_op jit(solution)/shard_map/dot_general | solution.py:42
  619.3 1.8 copy.14
  621.1 0.0 copy-done.1
Async XLA Ops:
  8.0 1.2 copy-start
  8.0 265.6 %reduce-scatter.2.cloned.1.call-start = ((), (), s32[]{:S(2)}) async-start(), calls=%async_computation.2 | async-start | bytes 35651584 | tf_op jit(solution)/shard_map/reduce_scatter | solution.py:28
  28.0 245.7 %copy-start.3 = (f32[1,512,1024]{2,1,0:T(8,128)S(1)}, f32[1,512,1024]{2,1,0:T(8,128)}, u32[]{:S(2)}) copy-start(f32[1,512,1024]{2,1,0:T(8,128)} %param.12) | copy-start | bytes 6291460
  286.4 9.6 %copy-start.2 = (f32[512,1024]{1,0:T(8,128)S(1)}, f32[512,1024]{1,0:T(8,128)}, u32[]{:S(2)}) copy-start(f32[512,1024]{1,0:T(8,128)} %param.14) | copy-start | bytes 6291460
  286.4 318.6 %all-to-all-start = ((bf16[16,512,1024]{2,1,0:T(8,128)(2,1)}), bf16[16,512,1024]{2,1,0:T(8,128)(2,1)}, u32[]{:S(2)}, u32[]{:S(2)}) async-start(bf16[16,512,1024]{2,1,0:T(8,128)(2,1)} %stack.2), calls=%async_computation.1 | async-start | bytes 33554432 | tf_op jit(solution)/shard_map/all_to_all | solution.py:45
  296.0 187.7 %all-reduce.2.cloned.1.call-start = ((), (), s32[]{:S(2)}) async-start(), calls=%async_computation.3 | async-start | bytes 4194304 | tf_op jit(solution)/shard_map/psum | solution.py:51
  605.0 16.2 %copy-start.1 = (bf16[1,512,1024]{2,1,0:T(8,128)(2,1)S(1)}, bf16[1,512,1024]{2,1,0:T(8,128)(2,1)}, u32[]{:S(2)}) copy-start(bf16[1,512,1024]{2,1,0:T(8,128)(2,1)} %param.9) | copy-start | bytes 3145732
Sparse Core Ops, SparseCore 0:
  28.1 245.5 reduce-scatter.1
Sparse Core Ops, SparseCore 1:
  299.5 184.1 all-reduce.1
